TPU v7x, 32 devices: a whole 2x2x4 slice. The times are simulated.
32 devices in a mesh: segment: 2 (over core), clip: 4 (over z), tile: 4 (over y, x).
Axes of the slice: x: 2, y: 2, z: 4, core: 2. Of those that a mesh axis runs over, the one named last changes fastest.
Arguments:
- video: bfloat16 [4, 4, 3, 12, 4, 256], P('clip', 'tile'), may hold values from -6 to 6
- cotangent: bfloat16 [4, 4, 3, 12, 4, 256], P('clip', 'tile'), may hold values from -6 to 6
- weights: bfloat16 [2, 27, 256, 256], P('segment'), may hold values from -0.078125 to 0.078125
- neighbours: int32 [4, 4, 2], P('clip', 'tile'), may hold values from 0 to 4, as said below
- rows_used: int32 [4, 4], P('clip', 'tile'), may hold values from 3 to 12, as said below
- cols_used: int32 [4], P('clip'), may hold values from 2 to 4, as said below
Outputs:
- section_out: bfloat16 [2, 4, 4, 3, 12, 4, 256], P('segment', 'clip', 'tile')
- grads: float32 [2, 3, 589824], P('segment', None, ('clip', 'tile'))
Inputs may be any that keep to these rules, and one draw needn't show every extreme that they name: `neighbours`: in each clip the strips of its frames lie on the 4 tiles in an order of their own: entry 0 names the tile of the strip above, entry 1 the tile of the strip below, 4 where there is none; exactly one strip of each clip has none above and one has none below, and the entries chain all 4 strips of a clip top to bottom. `rows_used`: in every clip some strip has 12 rows. `cols_used`: some clip has 4 columns.
All inputs are finite; a program needn't handle non-finite values.
Results may differ from a plain program's by a relative error of at most 0.0054.
Values may be sent and summed in bfloat16 or wider, within the bound.
A program may use at most 576 MiB of HBM per device.

v0:
```python
import jax
import jax.numpy as jnp
from jax import lax
from jax.sharding import PartitionSpec as P


def shifted(block, axis, distance):
    devices = range(lax.axis_size(axis))
    route = [(i - distance, i) for i in devices if i - distance in devices]
    return lax.ppermute(block, axis, route)


def silu_grad(values):
    sigmoid = jax.nn.sigmoid(values)
    return sigmoid * (1.0 + values * (1.0 - sigmoid))


def pad_block(strip_field, upper, bottom, row_count):
    frame_count, height, columns, channels = strip_field.shape
    blank = jnp.zeros((frame_count, 1, columns, channels), strip_field.dtype)
    padded = jnp.concatenate([upper[:, None], strip_field, blank], axis=1)
    padded = lax.dynamic_update_slice_in_dim(padded, bottom[:, None], row_count + 1, axis=1)
    return jnp.pad(padded, ((0, 0), (0, 0), (1, 1), (0, 0)))


def patches(stacked, frame_count, height, columns):
    pieces = []
    for depth_off in range(3):
        for row_off in range(3):
            for col_off in range(3):
                pieces.append(
                    stacked[
                        depth_off : depth_off + frame_count,
                        row_off : row_off + height,
                        col_off : col_off + columns,
                    ]
                )
    return jnp.concatenate(pieces, axis=-1).reshape(frame_count * height * columns, -1)


def every_tap_entries(patch_fwd, weighting, start, count, channels):
    span = 9 * channels
    row_total = min(count // channels + 2, span)
    row_low = jnp.minimum(start // channels, span - row_total)
    columns = jnp.concatenate(
        [
            lax.dynamic_slice_in_dim(patch_fwd, tap * span + row_low, row_total, 1)
            for tap in range(3)
        ],
        axis=1,
    )
    contract = (((0,), (0,)), ((), ()))
    block = lax.dot_general(
        columns, weighting, contract, preferred_element_type=jnp.float32
    ).reshape(3, -1)
    return block.T


def local(video, cotangent, weights, neighbours, rows_used, cols_used):
    window = video[0, 0]
    frame_count, height, columns, channels = window.shape
    tile_count = lax.axis_size("tile")
    section = lax.axis_index("segment")
    row_count = rows_used[0, 0]
    col_count = cols_used[0]
    upper_tile = neighbours[0, 0, 0]
    lower_tile = neighbours[0, 0, 1]
    row_ids = jnp.arange(height, dtype=jnp.int32)
    col_ids = jnp.arange(columns, dtype=jnp.int32)
    inside = (row_ids[:, None] < row_count) & (col_ids[None, :] < col_count)
    inside_mask = inside[None, :, :, None]
    kernel = weights[0]
    forward_mat = kernel.reshape(27 * channels, channels)
    backward_mat = kernel[::-1].transpose(0, 2, 1).reshape(27 * channels, channels)
    front_zero = jnp.zeros((2, height + 2, columns + 2, channels), jnp.bfloat16)

    def halo_block(field):
        leading = field[:, 0]
        trailing = lax.dynamic_index_in_dim(field, row_count - 1, axis=1, keepdims=False)
        both_rows = jnp.stack([leading, trailing], axis=1)
        gathered = lax.all_gather(both_rows[None], "tile", axis=0, tiled=True)
        upper = gathered[jnp.minimum(upper_tile, tile_count - 1), :, 1]
        bottom = gathered[jnp.minimum(lower_tile, tile_count - 1), :, 0]
        upper = jnp.where(upper_tile < tile_count, upper, jnp.zeros_like(upper))
        bottom = jnp.where(lower_tile < tile_count, bottom, jnp.zeros_like(bottom))
        return pad_block(field, upper, bottom, row_count)

    def advance(entry, history):
        count = entry.shape[0]
        activated = jax.nn.silu(entry.astype(jnp.float32)).astype(jnp.bfloat16)
        padded = halo_block(activated)
        stacked = jnp.concatenate([history, padded], axis=0)
        mixed = jnp.dot(
            patches(stacked, count, height, columns),
            forward_mat,
            preferred_element_type=jnp.float32,
        ).reshape(entry.shape)
        result = jnp.where(inside_mask, entry.astype(jnp.float32) + mixed, 0.0).astype(jnp.bfloat16)
        return (result, stacked[-2:], padded)

    source = jnp.where(inside_mask, window, jnp.zeros_like(window))
    is_encoder = section == 0
    first_out, first_hist, first_pad = advance(source, front_zero)
    latent = shifted(first_out, "segment", 1)
    second_out, second_hist, second_pad = advance(latent, front_zero)
    own_out = jnp.where(is_encoder, first_out, second_out)
    own_input = jnp.where(is_encoder, source, latent)
    own_pad = jnp.where(is_encoder, first_pad, second_pad)
    target = jnp.where(inside_mask, cotangent[0, 0], jnp.zeros_like(cotangent[0, 0]))
    patch_fwd = patches(
        jnp.concatenate([front_zero, own_pad], axis=0), frame_count, height, columns
    )
    back_stack = jnp.concatenate([halo_block(target), front_zero], axis=0)
    spread = jnp.dot(
        patches(back_stack, frame_count, height, columns),
        backward_mat,
        preferred_element_type=jnp.float32,
    ).reshape(target.shape)
    own_grad = jnp.where(
        inside_mask,
        target.astype(jnp.float32) + silu_grad(own_input.astype(jnp.float32)) * spread,
        0.0,
    ).astype(jnp.bfloat16)
    returned = shifted(own_grad, "segment", -1)
    weighting = jnp.where(is_encoder, returned, target).reshape(-1, channels)
    flat_rows = 9 * channels * channels // lax.axis_size(("clip", "tile"))
    shares = lax.psum_scatter(
        every_tap_entries(
            patch_fwd,
            weighting,
            jnp.int32(0),
            flat_rows * lax.axis_size(("clip", "tile")),
            channels,
        ),
        ("clip", "tile"),
        scatter_dimension=0,
        tiled=True,
    )
    summed = shares.T
    return (own_out[None, None, None], summed[None])


def solution(mesh):
    in_specs = (
        P("clip", "tile", None, None, None, None),
        P("clip", "tile", None, None, None, None),
        P("segment", None, None, None),
        P("clip", "tile", None),
        P("clip", "tile"),
        P("clip"),
    )
    out_specs = (
        P("segment", "clip", "tile", None, None, None, None),
        P("segment", None, ("clip", "tile")),
    )
    return jax.shard_map(local, mesh=mesh, in_specs=in_specs, out_specs=out_specs, check_vma=False)
```

profile of v0, /device:TPU:0, one launch (start us, length us, event | category | flops | bytes accessed | tf_op | source)
XLA Modules:
  0.0 367.3 jit_solution(6660135488782941422)
XLA Ops:
  7.2 0.0 all-reduce.10.cloned.1.call-start
  7.2 1.3 fusion.28
  12.4 0.1 broadcast_and_fusion
  12.5 1.0 bitcast_select_fusion
  13.5 1.0 fusion.18
  14.6 9.7 %all-gather.2 = bf16[12,2,4,256]{3,2,1,0:T(4,128)(2,1)S(1)} all-gather(bf16[3,2,4,256]{3,2,1,0:T(4,128)(2,1)S(1)} %copy.127), channel_id=4, replica_groups=mesh['segment'=2,'clip'=4,'tile'=4] {'tile'}, dimensions={0}, use_global_device_ids=true | all-gather | bytes 61440 | tf_op jit(solution)/shard_map/all_gather | solution.py:81
  24.4 8.2 %all-gather = bf16[12,2,4,256]{3,2,1,0:T(4,128)(2,1)S(1)} all-gather(bf16[3,2,4,256]{3,2,1,0:T(4,128)(2,1)S(1)} %copy.120), channel_id=2, replica_groups=mesh['segment'=2,'clip'=4,'tile'=4] {'tile'}, dimensions={0}, use_global_device_ids=true | all-gather | bytes 61440 | tf_op jit(solution)/shard_map/all_gather | solution.py:81
  32.7 0.1 pad.29.clone
  32.8 0.1 maximum_maximum_fusion.2
  32.9 0.1 dynamic_update_slice.9
  33.0 0.0 copy-start
  33.1 0.0 copy-start.2
  33.7 1.4 copy-done
  35.0 0.0 copy-done.2
  35.0 0.9 fusion.2
  35.9 1.3 collective-permute-start
  37.2 0.1 dynamic_update_slice.11
  37.4 5.7 %copy.130 = bf16[1,27,256,256]{2,3,1,0:T(8,128)(2,1)} copy(bf16[1,27,256,256]{3,2,1,0:T(8,128)(2,1)} %param.8) | data formatting | bytes 7077888 | tf_op args[2]
  43.7 0.0 copy-start.3
  43.7 4.2 %rev.3 = bf16[27,256,256]{1,2,0:T(8,128)(2,1)} reverse(bf16[27,256,256]{1,2,0:T(8,128)(2,1)} %bitcast.80), dimensions={0} | reverse | bytes 7077888 | tf_op jit(solution)/shard_map/rev | solution.py:74
  47.9 0.0 collective-permute-done
  48.0 0.0 copy-done.3
  48.0 3.0 fusion.14
  51.0 7.3 %all-gather.1 = bf16[12,2,4,256]{3,2,1,0:T(4,128)(2,1)S(1)} all-gather(bf16[3,2,4,256]{3,2,1,0:T(4,128)(2,1)S(1)} %copy.123), channel_id=3, replica_groups=mesh['segment'=2,'clip'=4,'tile'=4] {'tile'}, dimensions={0}, use_global_device_ids=true | all-gather | bytes 61440 | tf_op jit(solution)/shard_map/all_gather | solution.py:81
  58.3 0.1 maximum_maximum_fusion.1
  58.4 0.1 dynamic_update_slice.10
  59.2 1.5 collective-permute-start.1
  60.7 1.7 collective-permute-done.1
  62.4 4.0 %convolution_bitcast_fusion = f32[6912,256]{1,0:T(8,128)} fusion(bf16[3,12,4,6912]{3,1,2,0:T(8,128)(2,1)S(1)} %constant_dynamic-update-slice_fusion.54, bf16[3,12,4,256]{3,1,2,0:T(8,128)(2,1)S(1)} %collective-permute-done.1, pred[]{:T(512)S(6)} %eq.3, bf16[1,1,3,12,4,256]{5,4,3,2,1,0:T(4,128)(2,1)S(1)} %copy-done.3, pred[12,4]{0,1:T(4,128)(4,1)S(1)} %broadcast_and_fusion), kind=kOutput, calls=%fused_computation | convolution fusion | flops 509681664 | bytes 9216049 | tf_op jit(solution)/shard_map/dot_general | solution.py:53
  66.4 10.6 %reshape.152 = f32[3,589824]{1,0:T(4,128)} reshape(f32[6912,256]{1,0:T(8,128)} %convolution_bitcast_fusion) | data formatting | bytes 14155776 | tf_op jit(solution)/shard_map/reshape | solution.py:55
  77.0 0.0 copy-start.4
  77.0 0.0 all-reduce.10.cloned.1.call-update
  77.0 0.6 copy-done.4
  77.6 0.6 dynamic-slice
  78.9 0.0 copy-start.1
  79.5 1.4 copy-done.1
  80.9 0.9 fusion.5
  81.8 0.7 copy.131
  82.5 275.6 %all-reduce.10.cloned.1.call-done = f32[589824,3]{0,1:T(4,128)} async-done(((f32[589824,3]{0,1:T(4,128)}), f32[589824,3]{0,1:T(4,128)}) %all-reduce.10.cloned.1.call-update) | async-done | bytes 7077904
  358.1 1.2 dynamic-slice_bitcast_fusion
  359.2 1.2 copy.132
  (130 shorter events, 2.2 us)
Async XLA Ops:
  7.2 350.9 %all-reduce.10.cloned.1.call-start = ((), (), s32[]{:S(2)}) async-start(), calls=%async_computation | async-start | bytes 18874368
  33.0 2.0 copy-start
  33.1 2.0 copy-start.2
  35.9 12.0 %collective-permute-start = (bf16[3,12,4,256]{3,1,2,0:T(8,128)(2,1)S(1)}, bf16[3,12,4,256]{3,1,2,0:T(8,128)(2,1)S(1)}, u32[]{:S(2)}, u32[]{:S(2)}) collective-permute-start(bf16[3,12,4,256]{3,1,2,0:T(8,128)(2,1)S(1)} %fusion.2), channel_id=1, source_target_pairs={{0,16},{1,17},{2,18},{3,19},{4,20},{5,21},{6,22},{7,23},{8,24},{9,... | collective-permute-start | bytes 221192 | tf_op jit(solution)/shard_map/ppermute | solution.py:10
  43.7 4.2 %copy-start.3 = (bf16[1,1,3,12,4,256]{5,4,3,2,1,0:T(4,128)(2,1)S(1)}, bf16[1,1,3,12,4,256]{5,4,3,2,1,0:T(4,128)(2,1)}, u32[]{:S(2)}) copy-start(bf16[1,1,3,12,4,256]{5,4,3,2,1,0:T(4,128)(2,1)} %param.7) | copy-start | bytes 221188
  59.2 3.2 collective-permute-start.1
  77.0 0.7 copy-start.4
  78.9 2.0 copy-start.1
Sparse Core Ops, SparseCore 0:
  77.1 280.8 all-reduce.9
where the time goes:
time: 368 us; the launch traced here: 367 us
  waiting for transfers between devices  277 us (75%)
  local copies, waits for them, and re-layouts  31.2 us (8%)
  blocking collectives  25.2 us (7%)
  between operations  19.7 us (5%)
  matrix products  8.71 us (2%)
    unnamed x2, waiting for transfers between devices  276 us
    all_gather x3, blocking collectives, halo_block(): gathered = lax.all_gather(both_rows[None], 'tile', axis=0, tiled=True)  25.2 us
    unnamed x118, local copies, waits for them, and re-layouts  13.4 us
    reshape x1, local copies, waits for them, and re-layouts, every_tap_entries(): block = lax.dot_general(columns, weighting, contract, preferred_element_t...  10.6 us
  transfers between devices with their start and end apart: 3, of which 2 were waited for; matrix products, arithmetic and copies ran while one was open for 4% of the time, Pallas kernels for 0%

commit v1 on v0

--- a/solution.py
+++ b/solution.py
@@ -2,6 +2,13 @@
 import jax.numpy as jnp
 from jax import lax
 from jax.sharding import PartitionSpec as P
+
+
+def all_by_exchange(block, axis, along):
+    size = lax.axis_size(axis)
+    blocks = jnp.stack([block for _ in range(size)])
+    blocks = lax.all_to_all(blocks, axis, split_axis=0, concat_axis=0)
+    return jnp.concatenate(blocks, axis=along)
 
 
 def shifted(block, axis, distance):
@@ -78,7 +85,7 @@
         leading = field[:, 0]
         trailing = lax.dynamic_index_in_dim(field, row_count - 1, axis=1, keepdims=False)
         both_rows = jnp.stack([leading, trailing], axis=1)
-        gathered = lax.all_gather(both_rows[None], "tile", axis=0, tiled=True)
+        gathered = all_by_exchange(both_rows[None], "tile", 0)
         upper = gathered[jnp.minimum(upper_tile, tile_count - 1), :, 1]
         bottom = gathered[jnp.minimum(lower_tile, tile_count - 1), :, 0]
         upper = jnp.where(upper_tile < tile_count, upper, jnp.zeros_like(upper))

time: 368 us -> 361 us (0.981)
  blocking collectives: 25.2 us -> 0 us
  starting transfers between devices: 2.81 us -> 15.3 us
  waiting for transfers between devices: 277 us -> 283 us
    all_gather x3 -> x0, blocking collectives: 25.2 us -> none  [halo_block(): gathered = lax.all_gather(both_rows[None], 'tile', axis=0, tiled=True)]
    all_to_all x0 -> x3, starting transfers between devices: none -> 12.6 us  [all_by_exchange(): blocks = lax.all_to_all(blocks, axis, split_axis=0, concat_axis=0)]
    all_to_all x0 -> x3, waiting for transfers between devices: none -> 7.47 us  [all_by_exchange(): blocks = lax.all_to_all(blocks, axis, split_axis=0, concat_axis=0)]
    unnamed x118 -> x124, local copies, waits for them, and re-layouts: 13.4 us -> 13.3 us
  transfers between devices with their start and end apart: 3 -> 6, of which waited for: 2 -> 4; matrix products, arithmetic and copies ran while one was open for 4% -> 3% of each run, Pallas kernels for 0% -> 0%
where the time goes in v1:
time: 361 us; the launch traced here: 360 us
  waiting for transfers between devices  283 us (78%)
  local copies, waits for them, and re-layouts  31.1 us (9%)
  between operations  19.9 us (6%)
  starting transfers between devices  15.3 us (4%)
  matrix products  6.76 us (2%)
  other arithmetic  4.14 us (1%)
    unnamed x2, waiting for transfers between devices  275 us
    unnamed x124, local copies, waits for them, and re-layouts  13.3 us
    all_to_all x3, starting transfers between devices, all_by_exchange(): blocks = lax.all_to_all(blocks, axis, split_axis=0, concat_axis=0)  12.6 us
    reshape x1, local copies, waits for them, and re-layouts, every_tap_entries(): block = lax.dot_general(columns, weighting, contract, preferred_element_t...  10.6 us
    all_to_all x3, waiting for transfers between devices, all_by_exchange(): blocks = lax.all_to_all(blocks, axis, split_axis=0, concat_axis=0)  7.47 us
  transfers between devices with their start and end apart: 6, of which 4 were waited for; matrix products, arithmetic and copies ran while one was open for 3% of the time, Pallas kernels for 0%

profile of v1, /device:TPU:0, one launch (start us, length us, event | category | flops | bytes accessed | tf_op | source)
XLA Modules:
  0.0 359.8 jit_solution(14360478803120073272)
XLA Ops:
  8.5 0.1 broadcast_and_fusion
  8.6 1.0 bitcast_select_fusion
  9.5 0.0 copy-start.3
  9.5 1.1 fusion.18
  10.6 0.0 copy-start.4
  10.7 0.6 stack.26
  11.4 5.2 %all-to-all-start.2 = ((bf16[4,1,3,2,4,256]{5,4,2,3,1,0:T(4,128)(2,1)}), bf16[4,1,3,2,4,256]{5,4,2,3,1,0:T(4,128)(2,1)}, u32[]{:S(2)}, u32[]{:S(2)}) async-start(bf16[4,1,3,2,4,256]{5,4,2,3,1,0:T(4,128)(2,1)} %stack.26), calls=%async_computation.2 | async-start | bytes 98304 | tf_op jit(solution)/shard_map/all_to_all | solution.py:10
  16.6 1.4 fusion.28
  20.8 0.0 copy-done.3
  20.8 0.0 copy-done.4
  20.8 4.4 %copy.103 = bf16[1,27,256,256]{2,3,1,0:T(8,128)(2,1)S(1)} copy(bf16[1,27,256,256]{3,2,1,0:T(8,128)(2,1)} %param.8) | data formatting | bytes 7077888 | tf_op args[2]
  25.2 2.0 rev.3
  27.2 0.1 pad.29.clone
  27.3 0.0 all-to-all-done.2
  27.3 0.6 stack.22
  27.9 4.2 %all-to-all-start = ((bf16[4,1,3,2,4,256]{5,4,2,3,1,0:T(4,128)(2,1)}), bf16[4,1,3,2,4,256]{5,4,2,3,1,0:T(4,128)(2,1)S(1)}, u32[]{:S(2)}, u32[]{:S(2)}) async-start(bf16[4,1,3,2,4,256]{5,4,2,3,1,0:T(4,128)(2,1)} %stack.22), calls=%async_computation | async-start | bytes 98304 | tf_op jit(solution)/shard_map/all_to_all | solution.py:10
  32.1 0.7 select_bitcast_fusion
  32.9 4.0 %all-to-all-done = bf16[4,1,3,2,4,256]{5,4,2,3,1,0:T(4,128)(2,1)S(1)} async-done(((bf16[4,1,3,2,4,256]{5,4,2,3,1,0:T(4,128)(2,1)}), bf16[4,1,3,2,4,256]{5,4,2,3,1,0:T(4,128)(2,1)S(1)}, u32[]{:S(2)}, u32[]{:S(2)}) %all-to-all-start) | async-done | bytes 49184 | tf_op jit(solution)/shard_map/all_to_all | solution.py:10
  37.0 1.1 maximum_maximum_fusion.2
  38.0 0.1 dynamic_update_slice.11
  38.2 0.1 dynamic_update_slice.9
  38.3 0.0 copy-start
  38.3 0.0 copy-start.5
  39.0 1.4 copy-done
  40.3 0.0 copy-done.5
  40.3 0.9 fusion.2
  41.2 1.3 collective-permute-start
  42.6 0.0 copy-start.2
  42.6 0.0 copy-start.6
  43.2 0.3 collective-permute-done
  43.5 1.2 copy-done.2
  44.6 0.0 copy-done.6
  44.6 1.0 fusion.14
  45.7 0.6 stack.24
  46.3 3.3 all-to-all-start.1
  49.6 0.0 all-reduce.10.cloned.1.call-start
  49.7 1.3 collective-permute-start.1
  51.0 3.4 all-to-all-done.1
  54.4 0.1 maximum_maximum_fusion.1
  54.5 0.2 dynamic_update_slice.10
  55.5 0.0 collective-permute-done.1
  55.5 4.0 %convolution_bitcast_fusion = f32[6912,256]{1,0:T(8,128)} fusion(bf16[3,12,4,6912]{3,1,2,0:T(8,128)(2,1)S(1)} %constant_dynamic-update-slice_fusion.54, bf16[3,12,4,256]{3,1,2,0:T(8,128)(2,1)S(1)} %collective-permute-done.1, pred[]{:T(512)S(6)} %eq.3, bf16[1,1,3,12,4,256]{5,4,3,2,1,0:T(4,128)(2,1)S(1)} %copy-done.6, pred[12,4]{0,1:T(4,128)(4,1)S(1)} %broadcast_and_fusion), kind=kOutput, calls=%fused_computation | convolution fusion | flops 509681664 | bytes 9216049 | tf_op jit(solution)/shard_map/dot_general | solution.py:60
  59.5 10.6 %reshape.173 = f32[3,589824]{1,0:T(4,128)} reshape(f32[6912,256]{1,0:T(8,128)} %convolution_bitcast_fusion) | data formatting | bytes 14155776 | tf_op jit(solution)/shard_map/reshape | solution.py:62
  70.2 0.0 copy-start.7
  70.2 0.0 all-reduce.10.cloned.1.call-update
  70.2 0.6 copy-done.7
  70.8 0.6 dynamic-slice.6
  72.1 0.0 copy-start.1
  72.7 1.4 copy-done.1
  74.1 0.9 fusion.5
  75.0 0.7 copy.104
  75.7 274.9 %all-reduce.10.cloned.1.call-done = f32[589824,3]{0,1:T(4,128)} async-done(((f32[589824,3]{0,1:T(4,128)}), f32[589824,3]{0,1:T(4,128)}) %all-reduce.10.cloned.1.call-update) | async-done | bytes 7077904
  350.6 1.2 dynamic-slice_bitcast_fusion
  351.7 1.2 copy.105
  (129 shorter events, 2.2 us)
Async XLA Ops:
  9.5 11.2 %copy-start.3 = (bf16[3,12,4,256]{3,1,2,0:T(8,128)(2,1)}, bf16[3,12,4,256]{3,1,2,0:T(8,128)(2,1)S(1)}, u32[]{:S(2)}) copy-start(bf16[3,12,4,256]{3,1,2,0:T(8,128)(2,1)S(1)} %bitcast_select_fusion) | copy-start | bytes 221188
  10.6 10.2 %copy-start.4 = (bf16[3,12,4,256]{3,1,2,0:T(8,128)(2,1)}, bf16[3,12,4,256]{3,1,2,0:T(8,128)(2,1)S(1)}, u32[]{:S(2)}) copy-start(bf16[3,12,4,256]{3,1,2,0:T(8,128)(2,1)S(1)} %fusion.18) | copy-start | bytes 221188
  11.4 15.9 %all-to-all-start.2 = ((bf16[4,1,3,2,4,256]{5,4,2,3,1,0:T(4,128)(2,1)}), bf16[4,1,3,2,4,256]{5,4,2,3,1,0:T(4,128)(2,1)}, u32[]{:S(2)}, u32[]{:S(2)}) async-start(bf16[4,1,3,2,4,256]{5,4,2,3,1,0:T(4,128)(2,1)} %stack.26), calls=%async_computation.2 | async-start | bytes 98304 | tf_op jit(solution)/shard_map/all_to_all | solution.py:10
  27.9 9.0 %all-to-all-start = ((bf16[4,1,3,2,4,256]{5,4,2,3,1,0:T(4,128)(2,1)}), bf16[4,1,3,2,4,256]{5,4,2,3,1,0:T(4,128)(2,1)S(1)}, u32[]{:S(2)}, u32[]{:S(2)}) async-start(bf16[4,1,3,2,4,256]{5,4,2,3,1,0:T(4,128)(2,1)} %stack.22), calls=%async_computation | async-start | bytes 98304 | tf_op jit(solution)/shard_map/all_to_all | solution.py:10
  38.3 2.0 copy-start
  38.3 2.0 copy-start.5
  41.2 2.2 collective-permute-start
  42.6 2.0 copy-start.2
  42.6 2.0 copy-start.6
  46.3 8.1 %all-to-all-start.1 = ((bf16[4,1,3,2,4,256]{5,4,2,3,1,0:T(4,128)(2,1)}), bf16[4,1,3,2,4,256]{5,4,2,3,1,0:T(4,128)(2,1)S(1)}, u32[]{:S(2)}, u32[]{:S(2)}) async-start(bf16[4,1,3,2,4,256]{5,4,2,3,1,0:T(4,128)(2,1)} %stack.24), calls=%async_computation.1 | async-start | bytes 98304 | tf_op jit(solution)/shard_map/all_to_all | solution.py:10
  49.6 301.0 %all-reduce.10.cloned.1.call-start = ((), (), s32[]{:S(2)}) async-start(), calls=%async_computation.3 | async-start | bytes 18874368
  49.7 5.8 %collective-permute-start.1 = (bf16[3,12,4,256]{3,1,2,0:T(8,128)(2,1)S(1)}, bf16[3,12,4,256]{3,1,2,0:T(8,128)(2,1)S(1)}, u32[]{:S(2)}, u32[]{:S(2)}) collective-permute-start(bf16[3,12,4,256]{3,1,2,0:T(8,128)(2,1)S(1)} %get-tuple-element.18), channel_id=1, source_target_pairs={{16,0},{17,1},{18,2},{19,3},{20,4},{21,5},{22,6},{23,7},{24,8},{25... | collective-permute-start | bytes 221192 | tf_op jit(solution)/shard_map/ppermute | solution.py:17
  70.2 0.7 copy-start.7
  72.1 2.0 copy-start.1
Sparse Core Ops, SparseCore 0:
  70.3 280.2 all-reduce.9
